TPU v7x, 32 devices: a whole 2x2x4 slice. The times are simulated.
32 devices in a mesh: seq: 16 (over z, x, core), head: 2 (over y).
Axes of the slice: x: 2, y: 2, z: 4, core: 2. Of those that a mesh axis runs over, the one named last changes fastest.
Arguments:
- queries: bfloat16 [2, 1024, 4096], P(None, ('seq', 'head')), may hold values from -6 to 6
- keys: bfloat16 [2, 1024, 4096], P(None, ('seq', 'head')), may hold values from -6 to 6
- values: bfloat16 [2, 1024, 4096], P(None, ('seq', 'head')), may hold values from -6 to 6
- rates: bfloat16 [2, 1024, 8], P(None, ('seq', 'head')), may hold values from 0.049804688 to 1
- fast_init: float32 [8, 3, 512, 256], P('head', None, 'seq'), may hold values from -0.25 to 0.25
Outputs:
- outputs: bfloat16 [2, 1024, 4096], P(None, 'seq', 'head')
All inputs are finite; a program needn't handle non-finite values.
Results may differ from a plain program's by a relative error of at most 0.0085.
Values may be sent and summed in bfloat16 or wider, within the bound.
No kernel may reach another device: no remote copies, remote signals or barrier semaphores. Data moves between devices by JAX's collectives and lax.ppermute only.
A program may use at most 64 MiB of HBM per device.

v0:
```python
import jax
import jax.numpy as jnp
from jax import lax
from jax.sharding import PartitionSpec as P

EPSILON = 1e-06
COEF_A = 3.4445
COEF_B = -4.775
COEF_C = 2.0315
LEARNING_STEP = 0.5
FULL_PRECISION = lax.Precision.HIGHEST


def silu_parts(gate_pre):
    sigmoid_value = jax.nn.sigmoid(gate_pre)
    return (gate_pre * sigmoid_value, sigmoid_value * (1.0 + gate_pre * (1.0 - sigmoid_value)))


def local_gram(weight_matrices):
    return jnp.einsum("hmrf,hmrg->hmfg", weight_matrices, weight_matrices, precision=FULL_PRECISION)


def newton_schulz(gradients, gram_fn):
    gram_matrix = gram_fn(gradients)
    norm_value = jnp.sqrt(jnp.trace(gram_matrix, axis1=2, axis2=3)) + EPSILON
    current_weights = gradients / norm_value[:, :, None, None]
    gram_matrix = gram_matrix / (norm_value * norm_value)[:, :, None, None]
    identity = jnp.eye(gram_matrix.shape[-1], dtype=gram_matrix.dtype)
    for sweeps in range(2):
        if sweeps > 0:
            gram_matrix = gram_fn(current_weights)
        square = jnp.einsum("hmfg,hmgk->hmfk", gram_matrix, gram_matrix, precision=FULL_PRECISION)
        polynomial_update = COEF_A * identity + COEF_B * gram_matrix + COEF_C * square
        current_weights = jnp.einsum(
            "hmrf,hmfg->hmrg", current_weights, polynomial_update, precision=FULL_PRECISION
        )
    return current_weights


def local(queries, keys, values, rates, fast_init):
    weights = lax.all_gather(fast_init, "seq", axis=2, tiled=True)
    head_count = weights.shape[0]
    head_size = weights.shape[2]
    results = []
    for group_index in range(queries.shape[0]):
        query_flat, key_flat, value_flat, rate_rows = (
            lax.all_to_all(queries[group_index], "head", split_axis=1, concat_axis=0, tiled=True),
            lax.all_to_all(keys[group_index], "head", split_axis=1, concat_axis=0, tiled=True),
            lax.all_to_all(values[group_index], "head", split_axis=1, concat_axis=0, tiled=True),
            lax.all_to_all(rates[group_index], "head", split_axis=1, concat_axis=0, tiled=True),
        )
        row_count = query_flat.shape[0]
        query_rows = query_flat.reshape(row_count, head_count, head_size)
        key_rows = key_flat.reshape(row_count, head_count, head_size)
        value_rows = value_flat.reshape(row_count, head_count, head_size)
        low = weights.astype(jnp.bfloat16)
        gate_pre = jnp.einsum(
            "rhd,hdf->rhf", key_rows, low[:, 0], preferred_element_type=jnp.float32
        )
        up_proj = jnp.einsum(
            "rhd,hdf->rhf", key_rows, low[:, 1], preferred_element_type=jnp.float32
        )
        activated_hidden, slope_value = silu_parts(gate_pre)
        hidden = (activated_hidden * up_proj).astype(jnp.bfloat16)
        out_grad = (
            -(rate_rows.astype(jnp.float32)[:, :, None] * value_rows.astype(jnp.float32))
        ).astype(jnp.bfloat16)
        hidden_grad = jnp.einsum(
            "rhd,hdf->rhf", out_grad, low[:, 2], preferred_element_type=jnp.float32
        )
        gate_grad = (hidden_grad * up_proj * slope_value).astype(jnp.bfloat16)
        up_grad = (hidden_grad * activated_hidden).astype(jnp.bfloat16)
        gradients = jnp.stack(
            [
                jnp.einsum("rhd,rhf->hdf", key_rows, gate_grad, preferred_element_type=jnp.float32),
                jnp.einsum("rhd,rhf->hdf", key_rows, up_grad, preferred_element_type=jnp.float32),
                jnp.einsum("rhd,rhf->hdf", out_grad, hidden, preferred_element_type=jnp.float32),
            ],
            axis=1,
        )
        total_grad = lax.psum(gradients, "seq")
        update = newton_schulz(total_grad, local_gram)
        weights = weights - LEARNING_STEP * update
        low = weights.astype(jnp.bfloat16)
        query_gate = jnp.einsum(
            "rhd,hdf->rhf", query_rows, low[:, 0], preferred_element_type=jnp.float32
        )
        query_up = jnp.einsum(
            "rhd,hdf->rhf", query_rows, low[:, 1], preferred_element_type=jnp.float32
        )
        query_act, unused_slope = silu_parts(query_gate)
        query_hidden = (query_act * query_up).astype(jnp.bfloat16)
        result = jnp.einsum(
            "rhf,hdf->rhd", query_hidden, low[:, 2], preferred_element_type=jnp.float32
        )
        results.append(result.astype(jnp.bfloat16).reshape(row_count, head_count * head_size))
    return jnp.stack(results)


def solution(mesh):
    return jax.shard_map(
        local,
        mesh=mesh,
        in_specs=(
            P(None, ("seq", "head"), None),
            P(None, ("seq", "head"), None),
            P(None, ("seq", "head"), None),
            P(None, ("seq", "head"), None),
            P("head", None, "seq", None),
        ),
        out_specs=P(None, "seq", "head"),
        check_vma=False,
    )
```

profile of v0, /device:TPU:0, one launch (start us, length us, event | category | flops | bytes accessed | tf_op | source)
XLA Modules:
  0.0 496.7 jit_solution(14485534307048518920)
XLA Ops:
  9.7 4.3 all-to-all-start
  17.7 3.5 all-to-all-start.2
  22.2 4.1 all-to-all-done.2
  30.1 4.8 all-to-all-done.1
  35.5 38.2 %all-gather.2.cloned.1.call-done = f32[4,3,512,256]{3,2,0,1:T(8,128)} async-done(((f32[4,3,32,256]{3,2,0,1:T(8,128)}), f32[4,3,512,256]{3,2,0,1:T(8,128)}) %all-gather.2.cloned.1.call-update) | async-done | bytes 6291472 | tf_op jit(solution)/shard_map/all_gather | solution.py:41
  89.5 3.4 all-to-all-start.5
  93.0 5.1 %all-to-all-done.5 = bf16[32,2,2048]{2,0,1:T(8,128)(2,1)S(1)} async-done(((bf16[32,2,2048]{2,0,1:T(8,128)(2,1)}), bf16[32,2,2048]{2,0,1:T(8,128)(2,1)S(1)}, u32[]{:S(2)}, u32[]{:S(2)}) %all-to-all-start.5) | async-done | bytes 262176 | tf_op jit(solution)/shard_map/all_to_all | solution.py:49
  102.2 4.5 all-to-all-done.6
  108.5 112.3 %all-reduce.3.cloned.1.call-done = f32[4,3,512,256]{2,3,0,1:T(8,128)} async-done(((f32[4,3,512,256]{2,3,0,1:T(8,128)}), f32[4,3,512,256]{2,3,0,1:T(8,128)}) %all-reduce.3.cloned.1.call-update) | async-done | bytes 6291472 | tf_op jit(solution)/shard_map/psum | solution.py:81
  220.8 19.0 %select_reduce_fusion.1 = (f32[4,3]{1,0:T(4,128)S(1)}, f32[4,3,256,256]{3,2,1,0:T(8,128)}) fusion(pred[256,256]{1,0:T(8,128)(4,1)S(1)} %iota_compare_fusion, f32[4,3,512,256]{2,3,0,1:T(8,128)} %all-reduce.3.cloned.1.call-done), kind=kOutput, calls=%fused_computation.31 | convolution fusion | flops 4833411072 | bytes 9502768 | tf_op jit(solution)/shard_map/hmrf,hmrg->hmfg/dot_general | solution.py:20
  239.9 6.4 %fusion.36 = f32[4,3,256,256]{3,2,1,0:T(8,128)S(1)} fusion(f32[4,3,256,256]{3,2,1,0:T(8,128)} %get-tuple-element.18, f32[4,3]{1,0:T(4,128)S(1)} %get-tuple-element.15), kind=kOutput, calls=%fused_computation.46 | convolution fusion | flops 2416705536 | bytes 6291504 | tf_op jit(solution)/shard_map/hmfg,hmgk->hmfk/dot_general | solution.py:32
  246.4 10.8 %fusion.2 = f32[4,3,512,256]{3,2,1,0:T(8,128)S(1)} fusion(f32[4,3,256,256]{3,2,1,0:T(8,128)S(1)} %fusion.36, f32[256,256]{1,0:T(8,128)S(1)} %broadcast_select_fusion, f32[4,3,256,256]{3,2,1,0:T(8,128)S(1)} %copy-done.1, f32[4,3]{1,0:T(4,128)S(1)} %get-tuple-element.15, f32[4,3,512,256]{2,3,0,1:T(8,128)S(1)} %bitcast.117, f32[4,3]{0,1:T(4,128)S(1)} %copy.76), kind=kOutput, calls=%fused_computation.4 | convolution fusion | flops 4837343232 | bytes 19136608 | tf_op jit(solution)/shard_map/hmrf,hmfg->hmrg/dot_general | solution.py:34
  257.2 10.6 %fusion.101 = f32[4,3,256,256]{3,2,1,0:T(8,128)S(1)} fusion(f32[4,3,512,256]{3,2,1,0:T(8,128)S(1)} %fusion.2), kind=kOutput, calls=%fused_computation.145 | convolution fusion | flops 4831838208 | bytes 9437184 | tf_op jit(solution)/shard_map/hmrf,hmrg->hmfg/dot_general | solution.py:20
  267.9 3.9 multiply_add_fusion.1
  271.8 8.1 %fusion.100 = (bf16[4,3,512,256]{3,2,0,1:T(8,128)(2,1)S(1)}, f32[4,3,512,256]{3,2,0,1:T(8,128)}) fusion(f32[4,3,512,256]{3,2,0,1:T(8,128)S(1)} %bitcast.115, f32[4,3,256,256]{3,2,1,0:T(8,128)S(1)} %multiply_add_fusion.1, f32[4,3,512,256]{3,2,1,0:T(8,128)S(1)} %fusion.2), kind=kOutput, calls=%fused_computation.144 | convolution fusion | flops 4836556800 | bytes 25165824 | tf_op jit(solution)/shard_map/hmrf,hmfg->hmrg/dot_general | solution.py:34
  291.5 4.1 all-to-all-start.3
  300.9 4.1 all-to-all-start.7
  318.4 107.0 %all-reduce.5.cloned.1.call-done = f32[4,3,512,256]{2,3,0,1:T(8,128)} async-done(((f32[4,3,512,256]{2,3,0,1:T(8,128)}), f32[4,3,512,256]{2,3,0,1:T(8,128)}) %all-reduce.5.cloned.1.call-update) | async-done | bytes 6291472 | tf_op jit(solution)/shard_map/psum | solution.py:81
  425.5 18.8 %select_reduce_fusion = (f32[4,3]{1,0:T(4,128)S(1)}, f32[4,3,256,256]{3,2,1,0:T(8,128)}) fusion(pred[256,256]{1,0:T(8,128)(4,1)S(1)} %iota_compare_fusion, f32[4,3,512,256]{2,3,0,1:T(8,128)} %all-reduce.5.cloned.1.call-done), kind=kOutput, calls=%fused_computation.24 | convolution fusion | flops 4833411072 | bytes 9502768 | tf_op jit(solution)/shard_map/hmrf,hmrg->hmfg/dot_general | solution.py:20
  444.4 6.7 %fusion.37 = f32[4,3,256,256]{3,2,1,0:T(8,128)S(1)} fusion(f32[4,3,256,256]{3,2,1,0:T(8,128)} %get-tuple-element.22, f32[4,3]{1,0:T(4,128)S(1)} %get-tuple-element.13), kind=kOutput, calls=%fused_computation.47 | convolution fusion | flops 2416705536 | bytes 6291504 | tf_op jit(solution)/shard_map/hmfg,hmgk->hmfk/dot_general | solution.py:32
  451.1 11.4 %fusion = f32[4,3,512,256]{3,2,1,0:T(8,128)S(1)} fusion(f32[4,3,256,256]{3,2,1,0:T(8,128)S(1)} %fusion.37, f32[256,256]{1,0:T(8,128)S(1)} %broadcast_select_fusion, f32[4,3,256,256]{3,2,1,0:T(8,128)S(1)} %copy-done, f32[4,3]{1,0:T(4,128)S(1)} %get-tuple-element.13, f32[4,3,512,256]{2,3,0,1:T(8,128)S(1)} %bitcast.119, f32[4,3]{0,1:T(4,128)S(1)} %copy.97), kind=kOutput, calls=%fused_computation.2 | convolution fusion | flops 4837343232 | bytes 19136608 | tf_op jit(solution)/shard_map/hmrf,hmfg->hmrg/dot_general | solution.py:34
  462.6 10.8 %fusion.102 = f32[4,3,256,256]{3,2,1,0:T(8,128)S(1)} fusion(f32[4,3,512,256]{3,2,1,0:T(8,128)S(1)} %fusion), kind=kOutput, calls=%fused_computation.146 | convolution fusion | flops 4831838208 | bytes 9437184 | tf_op jit(solution)/shard_map/hmrf,hmrg->hmfg/dot_general | solution.py:20
  473.4 4.1 multiply_add_fusion
  477.6 6.5 %subtract_convert_fusion = bf16[4,3,512,256]{3,2,0,1:T(8,128)(2,1)S(1)} fusion(f32[4,3,512,256]{3,2,0,1:T(8,128)S(1)} %bitcast.113, f32[4,3,256,256]{3,2,1,0:T(8,128)S(1)} %multiply_add_fusion, f32[4,3,512,256]{3,2,1,0:T(8,128)S(1)} %fusion), kind=kOutput, calls=%fused_computation.14 | convolution fusion | flops 4836556800 | bytes 18874368 | tf_op jit(solution)/shard_map/hmrf,hmfg->hmrg/dot_general | solution.py:34
  (108 shorter events, 70.0 us)
Async XLA Ops:
  6.5 14.7 %copy-start.5 = (bf16[2,32,4096]{2,1,0:T(8,128)(2,1)S(1)}, bf16[2,32,4096]{2,1,0:T(8,128)(2,1)}, u32[]{:S(2)}) copy-start(bf16[2,32,4096]{2,1,0:T(8,128)(2,1)} %param.7) | copy-start | bytes 1572868
  6.5 67.2 %all-gather.2.cloned.1.call-start = ((), (), s32[]{:S(2)}) async-start(), calls=%async_computation.8 | async-start | bytes 6684672 | tf_op jit(solution)/shard_map/all_gather | solution.py:41
  9.7 8.0 %all-to-all-start = ((bf16[32,2,4]{0,2,1:T(4,128)(2,1)}), bf16[32,2,4]{0,2,1:T(4,128)(2,1)S(1)}, u32[]{:S(2)}, u32[]{:S(2)}) async-start(bf16[32,2,4]{0,2,1:T(4,128)(2,1)} %bitcast), calls=%async_computation | async-start | bytes 4096 | tf_op jit(solution)/shard_map/all_to_all | solution.py:50
  17.7 8.6 %all-to-all-start.2 = ((bf16[32,2,2048]{2,0,1:T(8,128)(2,1)}), bf16[32,2,2048]{2,0,1:T(8,128)(2,1)S(1)}, u32[]{:S(2)}, u32[]{:S(2)}) async-start(bf16[32,2,2048]{2,0,1:T(8,128)(2,1)} %copy.67), calls=%async_computation.2 | async-start | bytes 524288 | tf_op jit(solution)/shard_map/all_to_all | solution.py:48
  26.4 8.6 %all-to-all-start.1 = ((bf16[32,2,2048]{2,0,1:T(8,128)(2,1)}), bf16[32,2,2048]{2,0,1:T(8,128)(2,1)S(1)}, u32[]{:S(2)}, u32[]{:S(2)}) async-start(bf16[32,2,2048]{2,0,1:T(8,128)(2,1)} %copy.65), calls=%async_computation.1 | async-start | bytes 524288 | tf_op jit(solution)/shard_map/all_to_all | solution.py:49
  29.8 191.0 %all-reduce.3.cloned.1.call-start = ((), (), s32[]{:S(2)}) async-start(), calls=%async_computation.9 | async-start | bytes 12582912 | tf_op jit(solution)/shard_map/psum | solution.py:81
  82.6 6.8 %all-to-all-start.4 = ((bf16[32,2,4]{0,2,1:T(4,128)(2,1)}), bf16[32,2,4]{0,2,1:T(4,128)(2,1)S(1)}, u32[]{:S(2)}, u32[]{:S(2)}) async-start(bf16[32,2,4]{0,2,1:T(4,128)(2,1)} %bitcast.23), calls=%async_computation.4 | async-start | bytes 4096 | tf_op jit(solution)/shard_map/all_to_all | solution.py:50
  89.5 8.6 %all-to-all-start.5 = ((bf16[32,2,2048]{2,0,1:T(8,128)(2,1)}), bf16[32,2,2048]{2,0,1:T(8,128)(2,1)S(1)}, u32[]{:S(2)}, u32[]{:S(2)}) async-start(bf16[32,2,2048]{2,0,1:T(8,128)(2,1)} %copy.86), calls=%async_computation.5 | async-start | bytes 524288 | tf_op jit(solution)/shard_map/all_to_all | solution.py:49
  98.1 8.6 %all-to-all-start.6 = ((bf16[32,2,2048]{2,0,1:T(8,128)(2,1)}), bf16[32,2,2048]{2,0,1:T(8,128)(2,1)S(1)}, u32[]{:S(2)}, u32[]{:S(2)}) async-start(bf16[32,2,2048]{2,0,1:T(8,128)(2,1)} %copy.88), calls=%async_computation.6 | async-start | bytes 524288 | tf_op jit(solution)/shard_map/all_to_all | solution.py:48
  101.5 324.0 %all-reduce.5.cloned.1.call-start = ((), (), s32[]{:S(2)}) async-start(), calls=%async_computation.10 | async-start | bytes 12582912 | tf_op jit(solution)/shard_map/psum | solution.py:81
  220.8 25.5 %slice-start.4 = ((s8[6291456]{0:T(1024)(128)(4,1)}), s8[2097152]{0:T(1024)(128)(4,1)S(1)}, s32[]{:S(2)}) async-start(s8[6291456]{0:T(1024)(128)(4,1)} %bitcast.116), calls=%async_computation.15 | async-start | bytes 4194304
  239.9 6.4 %slice-start.5 = ((s8[6291456]{0:T(1024)(128)(4,1)}), s8[4194304]{0:T(1024)(128)(4,1)S(1)}, s32[]{:S(2)}) async-start(s8[6291456]{0:T(1024)(128)(4,1)} %bitcast.116), calls=%async_computation.16 | async-start | bytes 8388608
  239.9 6.4 %copy-start.1 = (f32[4,3,256,256]{3,2,1,0:T(8,128)S(1)}, f32[4,3,256,256]{3,2,1,0:T(8,128)}, u32[]{:S(2)}) copy-start(f32[4,3,256,256]{3,2,1,0:T(8,128)} %get-tuple-element.18) | copy-start | bytes 9437188
  239.9 31.8 %slice-start.2 = ((s8[6291456]{0:T(1024)(128)(4,1)}), s8[4194304]{0:T(1024)(128)(4,1)S(1)}, s32[]{:S(2)}) async-start(s8[6291456]{0:T(1024)(128)(4,1)} %bitcast.114), calls=%async_computation.13 | async-start | bytes 8388608
  246.4 25.4 %slice-start.3 = ((s8[6291456]{0:T(1024)(128)(4,1)}), s8[2097152]{0:T(1024)(128)(4,1)S(1)}, s32[]{:S(2)}) async-start(s8[6291456]{0:T(1024)(128)(4,1)} %bitcast.114), calls=%async_computation.14 | async-start | bytes 4194304
  271.8 8.1 %copy-start.2 = (bf16[64,4,512]{2,1,0:T(4,128)(2,1)S(1)}, bf16[64,4,512]{2,1,0:T(4,128)(2,1)}, u32[]{:S(2)}) copy-start(bf16[64,4,512]{2,1,0:T(4,128)(2,1)} %reshape.94) | copy-start | bytes 786436
  291.5 9.4 %all-to-all-start.3 = ((bf16[32,2,2048]{2,0,1:T(8,128)(2,1)}), bf16[32,2,2048]{2,0,1:T(8,128)(2,1)}, u32[]{:S(2)}, u32[]{:S(2)}) async-start(bf16[32,2,2048]{2,0,1:T(8,128)(2,1)} %copy.80), calls=%async_computation.3 | async-start | bytes 524288 | tf_op jit(solution)/shard_map/all_to_all | solution.py:47
  300.9 9.4 %all-to-all-start.7 = ((bf16[32,2,2048]{2,0,1:T(8,128)(2,1)}), bf16[32,2,2048]{2,0,1:T(8,128)(2,1)}, u32[]{:S(2)}, u32[]{:S(2)}) async-start(bf16[32,2,2048]{2,0,1:T(8,128)(2,1)} %copy.101), calls=%async_computation.7 | async-start | bytes 524288 | tf_op jit(solution)/shard_map/all_to_all | solution.py:47
  425.5 25.6 %slice-start.6 = ((s8[6291456]{0:T(1024)(128)(4,1)}), s8[2097152]{0:T(1024)(128)(4,1)S(1)}, s32[]{:S(2)}) async-start(s8[6291456]{0:T(1024)(128)(4,1)} %bitcast.118), calls=%async_computation.17 | async-start | bytes 4194304
  444.4 6.7 %slice-start.7 = ((s8[6291456]{0:T(1024)(128)(4,1)}), s8[4194304]{0:T(1024)(128)(4,1)S(1)}, s32[]{:S(2)}) async-start(s8[6291456]{0:T(1024)(128)(4,1)} %bitcast.118), calls=%async_computation.18 | async-start | bytes 8388608
  444.4 6.7 %copy-start = (f32[4,3,256,256]{3,2,1,0:T(8,128)S(1)}, f32[4,3,256,256]{3,2,1,0:T(8,128)}, u32[]{:S(2)}) copy-start(f32[4,3,256,256]{3,2,1,0:T(8,128)} %get-tuple-element.22) | copy-start | bytes 9437188
  444.4 33.2 %slice-start = ((s8[6291456]{0:T(1024)(128)(4,1)}), s8[4194304]{0:T(1024)(128)(4,1)S(1)}, s32[]{:S(2)}) async-start(s8[6291456]{0:T(1024)(128)(4,1)} %bitcast.112), calls=%async_computation.11 | async-start | bytes 8388608
  451.1 26.4 %slice-start.1 = ((s8[6291456]{0:T(1024)(128)(4,1)}), s8[2097152]{0:T(1024)(128)(4,1)S(1)}, s32[]{:S(2)}) async-start(s8[6291456]{0:T(1024)(128)(4,1)} %bitcast.112), calls=%async_computation.12 | async-start | bytes 4194304
  477.6 6.6 %copy-start.6 = (bf16[64,4,512]{2,1,0:T(4,128)(2,1)S(1)}, bf16[64,4,512]{2,1,0:T(4,128)(2,1)}, u32[]{:S(2)}) copy-start(bf16[64,4,512]{2,1,0:T(4,128)(2,1)} %reshape.95) | copy-start | bytes 786436
  (2 other events, 5.7 us)
Sparse Core Ops, SparseCore 0:
  9.5 64.1 all-gather.1
  82.7 137.9 all-reduce.2
  286.1 139.3 all-reduce.4
where the time goes:
time: 502 us; the launch traced here: 497 us
  waiting for transfers between devices  285 us (57%)
  matrix products  130 us (26%)
  starting transfers between devices  29.8 us (6%)
  local copies, waits for them, and re-layouts  26.7 us (5%)
  between operations  14.1 us (3%)
  other arithmetic  11.8 us (2%)
    psum x2, waiting for transfers between devices, local(): total_grad = lax.psum(gradients, 'seq')  219 us
    dot_general x4, matrix products, local_gram(): jnp.einsum('hmrf,hmrg->hmfg', weight_matrices, weight_matrices, precision...  59.2 us
    all_gather x1, waiting for transfers between devices, local(): weights = lax.all_gather(fast_init, 'seq', axis=2, tiled=True)  38.2 us
    dot_general x4, matrix products, newton_schulz(): jnp.einsum('hmrf,hmfg->hmrg', current_weights, polynomial_update, precisi...  36.9 us
    dot_general x4, matrix products, newton_schulz(): jnp.einsum('hmfg,hmgk->hmfk', gram_matrix, gram_matrix, precision=FULL_PR...  21.1 us
  transfers between devices with their start and end apart: 11, of which 11 were waited for; matrix products, arithmetic and copies ran while one was open for 5% of the time, Pallas kernels for 0%

commit v1 on v0

--- a/solution.py
+++ b/solution.py
@@ -78,7 +78,11 @@
             ],
             axis=1,
         )
-        total_grad = lax.psum(gradients, "seq")
+        total_grad = gradients
+        for hop in (1, 2, 4, 8):
+            total_grad = total_grad + lax.ppermute(
+                total_grad, "seq", [(dev, dev ^ hop) for dev in range(16)]
+            )
         update = newton_schulz(total_grad, local_gram)
         weights = weights - LEARNING_STEP * update
         low = weights.astype(jnp.bfloat16)

time: 502 us -> 1330 us (2.65)
  waiting for transfers between devices: 285 us -> 1120 us
  matrix products: 130 us -> 99.1 us
  other arithmetic: 11.8 us -> 36.1 us
    ppermute x0 -> x8, waiting for transfers between devices: none -> 1050 us  [local(): lax.ppermute(total_grad, 'seq', [(dev, dev ^ hop) for dev in range(16)])]
    psum x2 -> x0, waiting for transfers between devices: 219 us -> none  [local(): total_grad = lax.psum(gradients, 'seq')]
    add x0 -> x8, other arithmetic: none -> 28.5 us  [local(): total_grad + lax.ppermute(total_grad, 'seq', [(dev, dev ^ hop) for dev in...]
    dot_general x4, matrix products: 59.2 us -> 33.6 us  [local_gram(): jnp.einsum('hmrf,hmrg->hmfg', weight_matrices, weight_matrices, precision...]
  transfers between devices with their start and end apart: 11 -> 17, of which waited for: 11 -> 17; matrix products, arithmetic and copies ran while one was open for 5% -> 2% of each run, Pallas kernels for 0% -> 0%
where the time goes in v1:
time: 1330 us
  waiting for transfers between devices  1120 us (84%)
  matrix products  99.1 us (7%)
  other arithmetic  36.1 us (3%)
  starting transfers between devices  36 us (3%)
  local copies, waits for them, and re-layouts  25.7 us (2%)
  between operations  14.4 us (1%)
    ppermute x8, waiting for transfers between devices, local(): lax.ppermute(total_grad, 'seq', [(dev, dev ^ hop) for dev in range(16)])  1050 us
    all_gather x1, waiting for transfers between devices, local(): weights = lax.all_gather(fast_init, 'seq', axis=2, tiled=True)  38.3 us
    dot_general x4, matrix products, newton_schulz(): jnp.einsum('hmrf,hmfg->hmrg', current_weights, polynomial_update, precisi...  36.5 us
    dot_general x4, matrix products, local_gram(): jnp.einsum('hmrf,hmrg->hmfg', weight_matrices, weight_matrices, precision...  33.6 us
    add x8, other arithmetic, local(): total_grad + lax.ppermute(total_grad, 'seq', [(dev, dev ^ hop) for dev in...  28.5 us
  transfers between devices with their start and end apart: 17, of which 17 were waited for; matrix products, arithmetic and copies ran while one was open for 2% of the time, Pallas kernels for 0%

profile of v1, /device:TPU:0, one launch (start us, length us, event | category | flops | bytes accessed | tf_op | source)
XLA Modules:
  0.0 1326.3 jit_solution(11506815579728361066)
XLA Ops:
  29.9 4.9 all-to-all-done.1
  35.4 38.3 %all-gather.2.cloned.1.call-done = f32[4,3,512,256]{3,2,0,1:T(8,128)} async-done(((f32[4,3,32,256]{3,2,0,1:T(8,128)}), f32[4,3,512,256]{3,2,0,1:T(8,128)}) %all-gather.2.cloned.1.call-update) | async-done | bytes 6291472 | tf_op jit(solution)/shard_map/all_gather | solution.py:41
  80.3 9.9 collective-permute-done
  92.4 137.1 %collective-permute-done.1 = f32[4,3,512,256]{2,3,0,1:T(8,128)S(1)} collective-permute-done((f32[4,3,512,256]{2,3,0,1:T(8,128)S(1)}, f32[4,3,512,256]{2,3,0,1:T(8,128)S(1)}, u32[]{:S(2)}, u32[]{:S(2)}) %collective-permute-start.1) | collective-permute-done | bytes 6291488 | tf_op jit(solution)/shard_map/ppermute | solution.py:83
  233.5 135.3 %collective-permute-done.2 = f32[4,3,512,256]{2,3,0,1:T(8,128)S(1)} collective-permute-done((f32[4,3,512,256]{2,3,0,1:T(8,128)S(1)}, f32[4,3,512,256]{2,3,0,1:T(8,128)S(1)}, u32[]{:S(2)}, u32[]{:S(2)}) %collective-permute-start.2) | collective-permute-done | bytes 6291488 | tf_op jit(solution)/shard_map/ppermute | solution.py:83
  385.4 5.1 all-to-all-done.5
  394.5 4.7 all-to-all-done.6
  401.1 243.9 %collective-permute-done.3 = f32[4,3,512,256]{2,3,0,1:T(8,128)} collective-permute-done((f32[4,3,512,256]{2,3,0,1:T(8,128)}, f32[4,3,512,256]{2,3,0,1:T(8,128)}, u32[]{:S(2)}, u32[]{:S(2)}) %collective-permute-start.3) | collective-permute-done | bytes 6291488 | tf_op jit(solution)/shard_map/ppermute | solution.py:83
  645.0 6.2 add.111
  651.2 6.2 select_reduce_fusion.1
  661.7 10.6 fusion.2
  672.4 10.4 fusion.103
  686.9 8.1 fusion.102
  698.6 10.1 collective-permute-done.4
  710.8 137.0 %collective-permute-done.5 = f32[4,3,512,256]{2,3,0,1:T(8,128)S(1)} collective-permute-done((f32[4,3,512,256]{2,3,0,1:T(8,128)S(1)}, f32[4,3,512,256]{2,3,0,1:T(8,128)S(1)}, u32[]{:S(2)}, u32[]{:S(2)}) %collective-permute-start.5) | collective-permute-done | bytes 6291488 | tf_op jit(solution)/shard_map/ppermute | solution.py:83
  850.3 136.7 %collective-permute-done.6 = f32[4,3,512,256]{2,3,0,1:T(8,128)S(1)} collective-permute-done((f32[4,3,512,256]{2,3,0,1:T(8,128)S(1)}, f32[4,3,512,256]{2,3,0,1:T(8,128)S(1)}, u32[]{:S(2)}, u32[]{:S(2)}) %collective-permute-start.6) | collective-permute-done | bytes 6291488 | tf_op jit(solution)/shard_map/ppermute | solution.py:83
  1005.8 4.5 all-to-all-start.7
  1023.8 239.3 %collective-permute-done.7 = f32[4,3,512,256]{2,3,0,1:T(8,128)} collective-permute-done((f32[4,3,512,256]{2,3,0,1:T(8,128)}, f32[4,3,512,256]{2,3,0,1:T(8,128)}, u32[]{:S(2)}, u32[]{:S(2)}) %collective-permute-start.7) | collective-permute-done | bytes 6291488 | tf_op jit(solution)/shard_map/ppermute | solution.py:83
  1263.1 6.2 add.124
  1269.3 6.2 select_reduce_fusion
  1279.6 11.2 fusion
  1290.8 10.8 fusion.104
  1301.6 4.4 multiply_add_fusion
  1306.0 6.5 subtract_convert_fusion
  (120 shorter events, 118.2 us)
Async XLA Ops:
  6.5 14.5 %copy-start.6 = (bf16[2,32,4096]{2,1,0:T(8,128)(2,1)S(1)}, bf16[2,32,4096]{2,1,0:T(8,128)(2,1)}, u32[]{:S(2)}) copy-start(bf16[2,32,4096]{2,1,0:T(8,128)(2,1)} %param.7) | copy-start | bytes 1572868
  6.5 67.2 %all-gather.2.cloned.1.call-start = ((), (), s32[]{:S(2)}) async-start(), calls=%async_computation.8 | async-start | bytes 6684672 | tf_op jit(solution)/shard_map/all_gather | solution.py:41
  9.7 7.9 all-to-all-start
  17.6 8.6 all-to-all-start.2
  26.2 8.6 all-to-all-start.1
  80.0 10.2 collective-permute-start
  91.8 137.8 %collective-permute-start.1 = (f32[4,3,512,256]{2,3,0,1:T(8,128)S(1)}, f32[4,3,512,256]{2,3,0,1:T(8,128)S(1)}, u32[]{:S(2)}, u32[]{:S(2)}) collective-permute-start(f32[4,3,512,256]{2,3,0,1:T(8,128)S(1)} %fusion.97), channel_id=1, source_target_pairs={{0,4},{2,6},{4,0},{6,2},{8,12},{10,14},{12,8},{14,10},{16,20},{18,... | collective-permute-start | bytes 18874376 | tf_op jit(solution)/shard_map/ppermute | solution.py:83
  231.9 136.9 %collective-permute-start.2 = (f32[4,3,512,256]{2,3,0,1:T(8,128)S(1)}, f32[4,3,512,256]{2,3,0,1:T(8,128)S(1)}, u32[]{:S(2)}, u32[]{:S(2)}) collective-permute-start(f32[4,3,512,256]{2,3,0,1:T(8,128)S(1)} %fusion.114), channel_id=1, source_target_pairs={{0,8},{2,10},{4,12},{6,14},{8,0},{10,2},{12,4},{14,6},{16,24},{18,... | collective-permute-start | bytes 18874376 | tf_op jit(solution)/shard_map/ppermute | solution.py:83
  373.0 272.0 %collective-permute-start.3 = (f32[4,3,512,256]{2,3,0,1:T(8,128)}, f32[4,3,512,256]{2,3,0,1:T(8,128)}, u32[]{:S(2)}, u32[]{:S(2)}) collective-permute-start(f32[4,3,512,256]{2,3,0,1:T(8,128)} %add.110), channel_id=1, source_target_pairs={{0,16},{2,18},{4,20},{6,22},{8,24},{10,26},{12,28},{14,30},{16,0},... | collective-permute-start | bytes 18874376 | tf_op jit(solution)/shard_map/ppermute | solution.py:83
  374.9 6.9 all-to-all-start.4
  381.9 8.6 all-to-all-start.5
  390.5 8.8 all-to-all-start.6
  657.5 29.4 %slice-start.2 = ((s8[6291456]{0:T(1024)(128)(4,1)}), s8[4194304]{0:T(1024)(128)(4,1)S(1)}, s32[]{:S(2)}) async-start(s8[6291456]{0:T(1024)(128)(4,1)} %bitcast.114), calls=%async_computation.11 | async-start | bytes 8388608
  661.7 25.2 %slice-start.3 = ((s8[6291456]{0:T(1024)(128)(4,1)}), s8[2097152]{0:T(1024)(128)(4,1)S(1)}, s32[]{:S(2)}) async-start(s8[6291456]{0:T(1024)(128)(4,1)} %bitcast.114), calls=%async_computation.12 | async-start | bytes 4194304
  686.9 8.1 copy-start.4
  698.5 10.2 collective-permute-start.4
  710.3 137.6 %collective-permute-start.5 = (f32[4,3,512,256]{2,3,0,1:T(8,128)S(1)}, f32[4,3,512,256]{2,3,0,1:T(8,128)S(1)}, u32[]{:S(2)}, u32[]{:S(2)}) collective-permute-start(f32[4,3,512,256]{2,3,0,1:T(8,128)S(1)} %fusion.96), channel_id=1, source_target_pairs={{0,4},{2,6},{4,0},{6,2},{8,12},{10,14},{12,8},{14,10},{16,20},{18,... | collective-permute-start | bytes 18874376 | tf_op jit(solution)/shard_map/ppermute | solution.py:83
  850.2 141.8 %copy-start.7 = (bf16[2,32,4096]{2,1,0:T(8,128)(2,1)S(1)}, bf16[2,32,4096]{2,1,0:T(8,128)(2,1)}, u32[]{:S(2)}) copy-start(bf16[2,32,4096]{2,1,0:T(8,128)(2,1)} %param.5) | copy-start | bytes 1572868
  850.2 136.8 %collective-permute-start.6 = (f32[4,3,512,256]{2,3,0,1:T(8,128)S(1)}, f32[4,3,512,256]{2,3,0,1:T(8,128)S(1)}, u32[]{:S(2)}, u32[]{:S(2)}) collective-permute-start(f32[4,3,512,256]{2,3,0,1:T(8,128)S(1)} %fusion.113), channel_id=1, source_target_pairs={{0,8},{2,10},{4,12},{6,14},{8,0},{10,2},{12,4},{14,6},{16,24},{18,... | collective-permute-start | bytes 18874376 | tf_op jit(solution)/shard_map/ppermute | solution.py:83
  991.2 271.9 %collective-permute-start.7 = (f32[4,3,512,256]{2,3,0,1:T(8,128)}, f32[4,3,512,256]{2,3,0,1:T(8,128)}, u32[]{:S(2)}, u32[]{:S(2)}) collective-permute-start(f32[4,3,512,256]{2,3,0,1:T(8,128)} %add.123), channel_id=1, source_target_pairs={{0,16},{2,18},{4,20},{6,22},{8,24},{10,26},{12,28},{14,30},{16,0},... | collective-permute-start | bytes 18874376 | tf_op jit(solution)/shard_map/ppermute | solution.py:83
  996.4 9.4 all-to-all-start.3
  1005.8 9.7 all-to-all-start.7
  1275.6 30.4 %slice-start = ((s8[6291456]{0:T(1024)(128)(4,1)}), s8[4194304]{0:T(1024)(128)(4,1)S(1)}, s32[]{:S(2)}) async-start(s8[6291456]{0:T(1024)(128)(4,1)} %bitcast.112), calls=%async_computation.9 | async-start | bytes 8388608
  1279.6 26.4 %slice-start.1 = ((s8[6291456]{0:T(1024)(128)(4,1)}), s8[2097152]{0:T(1024)(128)(4,1)S(1)}, s32[]{:S(2)}) async-start(s8[6291456]{0:T(1024)(128)(4,1)} %bitcast.112), calls=%async_computation.10 | async-start | bytes 4194304
  (6 other events, 28.1 us)
Sparse Core Ops, SparseCore 0:
  9.5 64.1 all-gather.1
